TPU v7x, 128 devices: a whole 4x4x4 slice. The times are simulated.
128 devices in a mesh: ping: 16 (over x, z), band: 8 (over y, core).
Axes of the slice: x: 4, y: 4, z: 4, core: 2. Of those that a mesh axis runs over, the one named last changes fastest.
Arguments:
- echoes: bfloat16 [2048, 8, 2, 8192], P(('ping', 'band')), may hold values from -6 to 6
- replica: bfloat16 [8, 2, 128], replicated, may hold values from -0.375 to 0.375
- steering: bfloat16 [2, 64, 64], replicated, may hold values from -0.5 to 0.5
- angle_weights: bfloat16 [2, 128, 64], replicated, may hold values from -0.75 to 0.75
- range_weights: bfloat16 [64, 384, 128], P('band'), may hold values from -0.3125 to 0.3125
- range_offsets: int32 [64], P('band'), may hold values from 0 to 5
- merge_owner: int32 [256], replicated, may hold values from -1 to 15, as said below
- merge_slot: int32 [256], replicated, may hold values from 0 to 7
Outputs:
- merged: bfloat16 [128, 2, 128, 8192], P('ping', None, None, 'band')
Inputs may be any that keep to these rules, and one draw needn't show every extreme that they name: `merge_owner`: -1 marks a block that is not kept. Among the 16 blocks of one ping index (aligned blocks of the list) at most 2 name the same owner, and in every draw one owner is named by exactly 2 blocks of every ping index.
All inputs are finite; a program needn't handle non-finite values.
Results may differ from a plain program's by a relative error of at most 0.007.
Values may be sent and summed in bfloat16 or wider, within the bound.
No kernel may reach another device: no remote copies, remote signals or barrier semaphores. Data moves between devices by JAX's collectives and lax.ppermute only.
A program may use at most 128 MiB of HBM per device.

v0:
```python
import jax
import jax.numpy as jnp
from jax import lax
from jax.sharding import PartitionSpec as P

SUB_PINGS = 8


def toeplitz_blocks(replica):
    taps_count = replica.shape[2]
    shifts = jnp.arange(taps_count)
    row_index = jnp.arange(taps_count)[:, None]
    col_index = jnp.arange(taps_count)[None, :]
    lower_sel = ((row_index - col_index)[None] == shifts[:, None, None]).astype(jnp.float32)
    upper_sel = ((row_index - col_index + taps_count)[None] == shifts[:, None, None]).astype(
        jnp.float32
    )
    real_taps = replica[:, 0].astype(jnp.float32)
    imag_taps = replica[:, 1].astype(jnp.float32)
    high = lax.Precision.HIGHEST
    lower_real = jnp.einsum("ck,kmn->cmn", real_taps, lower_sel, precision=high)
    lower_imag = jnp.einsum("ck,kmn->cmn", imag_taps, lower_sel, precision=high)
    upper_real = jnp.einsum("ck,kmn->cmn", real_taps, upper_sel, precision=high)
    upper_imag = jnp.einsum("ck,kmn->cmn", imag_taps, upper_sel, precision=high)
    layers = [
        jnp.concatenate([lower_real, -lower_imag], 2),
        jnp.concatenate([lower_imag, lower_real], 2),
        jnp.concatenate([upper_real, -upper_imag], 2),
        jnp.concatenate([upper_imag, upper_real], 2),
    ]
    return jnp.concatenate(layers, 1).astype(jnp.bfloat16)


def compress(echo_part, toeplitz):
    pings, chans, parts, bins = echo_part.shape
    taps_count = toeplitz.shape[2] // 2
    block_count = bins // taps_count
    shaped = echo_part.reshape(pings, chans, parts, block_count, taps_count)
    weights = toeplitz.reshape(chans, 2, parts, taps_count, 2, taps_count)
    lower = jnp.einsum(
        "pcqbk,cqkon->pcobn", shaped, weights[:, 0], preferred_element_type=jnp.float32
    )
    upper = jnp.einsum(
        "pcqbk,cqkon->pcobn", shaped, weights[:, 1], preferred_element_type=jnp.float32
    )
    moved = jnp.concatenate([upper[:, :, :, 1:], jnp.zeros_like(upper[:, :, :, :1])], axis=3)
    total = lower + moved
    return total.reshape(pings, chans, 2, bins).astype(jnp.bfloat16)


def beamform(tile, steering, sub_pings):
    pings, chans, parts, bins = tile.shape
    blocks = pings // sub_pings
    grouped = tile.reshape(blocks, sub_pings * chans * parts, bins)
    real_steer = steering[0]
    imag_steer = steering[1]
    beam_count = real_steer.shape[0]
    mixer = jnp.concatenate(
        [
            jnp.concatenate([real_steer, -imag_steer], 1),
            jnp.concatenate([imag_steer, real_steer], 1),
        ],
        0,
    )
    mixer = (
        mixer.reshape(2 * beam_count, 2, sub_pings * chans)
        .transpose(0, 2, 1)
        .reshape(2 * beam_count, -1)
    )
    beams = jnp.einsum("yx,bxr->byr", mixer, grouped, preferred_element_type=jnp.float32)
    return beams.reshape(blocks, 2, beam_count, bins).astype(jnp.bfloat16)


def rotate_angles(beam_image, angle_weights, parity):
    matrices = jnp.where(parity[:, None, None] == 1, angle_weights[1], angle_weights[0])
    turned = jnp.einsum("bya,bpar->bpyr", matrices, beam_image, preferred_element_type=jnp.float32)
    return turned.astype(jnp.bfloat16)


def dense_interp(range_weights, range_offsets):
    count = range_weights.shape[0]
    selector = (
        jnp.arange(count)[None, None, :]
        == (range_offsets[:, None] + jnp.arange(3)[None, :])[:, :, None]
    ).astype(jnp.bfloat16)
    pieces = range_weights.reshape(count, 3, 128, 128)
    dense = jnp.einsum("jtb,jtin->bijn", selector, pieces, preferred_element_type=jnp.float32)
    return dense.astype(jnp.bfloat16).reshape(count * 128, count * 128)


def range_interp(turned, dense):
    flat = turned.reshape(-1, turned.shape[3])
    product = jnp.dot(flat, dense, preferred_element_type=jnp.float32)
    return product.astype(jnp.bfloat16).reshape(turned.shape)


def pack_rows(packer, source):
    flat = jnp.dot(packer, source.reshape(source.shape[0], -1), preferred_element_type=jnp.float32)
    return flat.astype(jnp.bfloat16).reshape((packer.shape[0],) + source.shape[1:])


def on_device(
    echoes, replica, steering, angle_weights, range_weights, range_offsets, merge_owner, merge_slot
):
    ping_count = lax.axis_size("ping")
    ping_index = lax.axis_index("ping")
    toeplitz = toeplitz_blocks(replica)
    compressed = compress(echoes, toeplitz)
    band_tile = lax.all_to_all(compressed, "band", split_axis=3, concat_axis=0, tiled=True)
    beam_image = beamform(band_tile, steering, SUB_PINGS)
    blocks_here = beam_image.shape[0]
    capacity = max(2, (blocks_here + ping_count - 1) // ping_count)
    slot_count = blocks_here // 2
    routes = merge_owner.reshape(ping_count, blocks_here)
    slots_all = merge_slot.reshape(ping_count, blocks_here)
    my_routes = lax.dynamic_index_in_dim(routes, ping_index, 0, keepdims=False)
    target_hot = (my_routes[:, None] == jnp.arange(ping_count)[None, :]).astype(jnp.int32)
    rank_send = jnp.sum(jnp.cumsum(target_hot, 0) * target_hot, 1) - 1
    packer = (target_hot.T[:, None, :] == 1) & (
        rank_send[None, None, :] == jnp.arange(capacity)[None, :, None]
    )
    packer = packer.reshape(ping_count * capacity, blocks_here).astype(jnp.bfloat16)
    owned = (routes == ping_index).astype(jnp.int32)
    rank_recv = jnp.cumsum(owned, 1) * owned - 1
    matched = (owned[:, None, :] == 1) & (
        rank_recv[:, None, :] == jnp.arange(capacity)[None, :, None]
    )
    matched_float = matched.astype(jnp.float32)
    slot_hot = (slots_all[:, :, None] == jnp.arange(slot_count)[None, None, :]).astype(jnp.float32)
    combiner = jnp.einsum("scb,sbo->osc", matched_float, slot_hot).reshape(
        slot_count, ping_count * capacity
    )
    combiner = combiner.astype(jnp.bfloat16)
    dense = dense_interp(range_weights, range_offsets)
    my_parity = (ping_index * blocks_here + jnp.arange(blocks_here)) % 2
    images = range_interp(rotate_angles(beam_image, angle_weights, my_parity), dense)
    outgoing = pack_rows(packer, images)
    arrived = lax.all_to_all(outgoing, "ping", split_axis=0, concat_axis=0, tiled=True)
    merged = jnp.dot(
        combiner, arrived.reshape(arrived.shape[0], -1), preferred_element_type=jnp.float32
    )
    return merged.reshape((slot_count,) + arrived.shape[1:]).astype(jnp.bfloat16)


def solution(mesh):
    placed = (
        P(("ping", "band"), None, None, None),
        P(),
        P(),
        P(),
        P("band", None, None),
        P("band"),
        P(),
        P(),
    )
    return jax.shard_map(
        on_device,
        mesh=mesh,
        in_specs=placed,
        out_specs=P("ping", None, None, "band"),
        check_vma=False,
    )
```

profile of v0, /device:TPU:68, one launch (start us, length us, event | category | flops | bytes accessed | tf_op | source)
XLA Modules:
  0.0 673.8 jit_solution(3247890180094275025)
XLA Ops:
  4.8 1.4 fusion.30
  6.3 9.8 %maximum_maximum_fusion = bf16[8,512,256]{2,0,1:T(8,128)(2,1)S(1)} fusion(bf16[8,128,128]{2,0,1:T(8,128)(2,1)S(1)} %fusion.27, bf16[8,128,128]{2,0,1:T(8,128)(2,1)S(1)} %get-tuple-element.21, bf16[8,128,128]{2,0,1:T(8,128)(2,1)S(1)} %get-tuple-element.22, bf16[8,128,128]{2,0,1:T(8,128)(2,1)S(1)} %fusion.28, bf16[8,128,128]{2,0,1:T(8,128)(2,1)S(1)} %get-tuple-element.10, ...), kind=kLoop, calls=%fused_computation.26 | loop fusion | flops 16777216 | bytes 3670016 | tf_op jit(solution)/shard_map/concatenate | solution.py:31
  16.5 7.8 %reshape.188 = bf16[16,8,2,64,128]{4,3,2,1,0:T(8,128)(2,1)} reshape(bf16[16,8,2,8192]{3,2,1,0:T(2,128)(2,1)} %param.8) | data formatting | bytes 8388608 | tf_op jit(solution)/shard_map/reshape | solution.py:38
  24.3 6.7 fusion.15
  31.0 4.7 slice.38
  35.6 2.9 fusion.2
  38.6 48.6 %copy.68 = bf16[16,8,2,64,128]{0,2,1,4,3:T(2,128)(2,1)} copy(bf16[16,8,2,64,128]{4,3,0,2,1:T(8,128)(2,1)} %fusion.2) | data formatting | bytes 8388608 | tf_op jit(solution)/shard_map/convert_element_type | solution.py:48
  87.2 37.8 %reshape.209 = bf16[8,2,131072]{2,1,0:T(2,128)(2,1)} reshape(bf16[8192,8,2,16]{3,2,1,0:T(2,128)(2,1)} %bitcast.128) | data formatting | bytes 8388608
  125.1 4.7 all-to-all-start
  131.5 2.7 copy.49
  134.7 44.8 %all-to-all-done = bf16[8,2,131072]{2,1,0:T(2,128)(2,1)} async-done(((bf16[8,2,131072]{2,1,0:T(2,128)(2,1)}), bf16[8,2,131072]{2,1,0:T(2,128)(2,1)}, u32[]{:S(2)}, u32[]{:S(2)}) %all-to-all-start) | async-done | bytes 4194336 | tf_op jit(solution)/shard_map/all_to_all | solution.py:109
  179.4 25.7 %reshape.210 = bf16[8192,8,2,16]{3,2,1,0:T(2,128)(2,1)} reshape(bf16[8,2,131072]{2,1,0:T(2,128)(2,1)} %all-to-all-done) | data formatting | bytes 8388608
  205.2 76.8 %copy.43 = bf16[16,8,2,8,1024]{4,2,1,0,3:T(2,128)(2,1)} copy(bf16[16,8,2,8,1024]{0,2,1,4,3:T(2,128)(2,1)} %bitcast.129) | data formatting | bytes 8388608 | tf_op jit(solution)/shard_map/all_to_all | solution.py:109
  282.0 7.2 %reshape.189 = bf16[16,128,1024]{2,1,0:T(8,128)(2,1)} reshape(bf16[8,16,8,2,1024]{4,3,2,1,0:T(2,128)(2,1)} %bitcast.132) | data formatting | bytes 8388608 | tf_op jit(solution)/shard_map/reshape | solution.py:54
  289.2 3.7 convolution_convert_fusion.3
  292.9 2.4 convolution_convert_fusion.2
  295.4 12.4 %convolution_convert_fusion.1 = bf16[4096,1024]{1,0:T(8,128)(2,1)} fusion(bf16[4096,1024]{1,0:T(8,128)(2,1)S(1)} %bitcast.134, bf16[128,8,8,128]{3,2,1,0:T(8,128)(2,1)} %bitcast.136), kind=kOutput, calls=%fused_computation.11 | convolution fusion | flops 8594128896 | bytes 18874368 | tf_op jit(solution)/shard_map/dot_general | solution.py:93
  307.8 8.1 %reshape_reshape.3 = bf16[16,262144]{1,0:T(8,128)(2,1)} reshape(bf16[4096,1024]{1,0:T(8,128)(2,1)} %convolution_convert_fusion.1) | data formatting | bytes 16777216 | tf_op jit(solution)/shard_map/reshape;reshape | solution.py:98
  316.0 13.6 %convolution_convert_fusion = bf16[32,262144]{1,0:T(8,128)(2,1)} fusion(pred[32,16]{1,0:T(32,128)(4,1)S(1)} %and.49, bf16[16,262144]{1,0:T(8,128)(2,1)} %reshape_reshape.3), kind=kOutput, calls=%fused_computation | convolution fusion | flops 276824064 | bytes 25166336 | tf_op jit(solution)/shard_map/dot_general | solution.py:98
  329.5 18.7 %copy.77 = bf16[4,8,256,1024]{3,2,1,0:T(8,128)(2,1)} copy(bf16[4,8,256,1024]{3,1,2,0:T(8,128)(2,1)} %bitcast.131) | data formatting | bytes 33554432
  348.3 7.9 %all-to-all-start.1 = ((bf16[32,2,128,1024]{3,2,1,0:T(8,128)(2,1)}), bf16[32,2,128,1024]{3,2,1,0:T(8,128)(2,1)}, u32[]{:S(2)}, u32[]{:S(2)}) async-start(bf16[32,2,128,1024]{3,2,1,0:T(8,128)(2,1)} %bitcast.130), calls=%async_computation.1 | async-start | bytes 33554432 | tf_op jit(solution)/shard_map/all_to_all | solution.py:138
  356.6 295.7 %all-to-all-done.1 = bf16[32,2,128,1024]{3,2,1,0:T(8,128)(2,1)} async-done(((bf16[32,2,128,1024]{3,2,1,0:T(8,128)(2,1)}), bf16[32,2,128,1024]{3,2,1,0:T(8,128)(2,1)}, u32[]{:S(2)}, u32[]{:S(2)}) %all-to-all-start.1) | async-done | bytes 16777248 | tf_op jit(solution)/shard_map/all_to_all | solution.py:138
  652.3 16.6 %fusion.20 = bf16[8,2,128,1024]{3,0,2,1:T(8,128)(2,1)S(1)} fusion(bf16[8,32,1,1]{0,1,3,2:T(8,128)(2,1)S(1)} %bitcast.141, bf16[2,128,1024,32]{2,1,0,3:T(8,128)(2,1)} %bitcast.76), kind=kOutput, calls=%fused_computation.22 | convolution fusion | flops 136314880 | bytes 20972032 | tf_op jit(solution)/shard_map/dot_general | solution.py:139
  669.0 4.4 copy.52
  (48 shorter events, 7.7 us)
Async XLA Ops:
  0.0 130.3 %copy-start = (bf16[8,384,128]{2,1,0:T(8,128)(2,1)S(1)}, bf16[8,384,128]{2,1,0:T(8,128)(2,1)}, u32[]{:S(2)}) copy-start(bf16[8,384,128]{2,1,0:T(8,128)(2,1)} %param.12) | copy-start | bytes 2359300
  31.0 4.7 copy-start.2
  125.1 4.7 copy-start.3
  125.1 5.1 copy-start.7
  125.1 54.4 %all-to-all-start = ((bf16[8,2,131072]{2,1,0:T(2,128)(2,1)}), bf16[8,2,131072]{2,1,0:T(2,128)(2,1)}, u32[]{:S(2)}, u32[]{:S(2)}) async-start(bf16[8,2,131072]{2,1,0:T(2,128)(2,1)} %reshape.209), calls=%async_computation | async-start | bytes 8388608 | tf_op jit(solution)/shard_map/all_to_all | solution.py:109
  129.8 4.4 copy-start.5
  129.8 4.8 copy-start.4
  348.3 8.1 %copy-start.6 = (s32[256]{0:T(256)S(1)}, s32[256]{0:T(256)}, u32[]{:S(2)}) copy-start(s32[256]{0:T(256)} %param.15) | copy-start | bytes 3076
  348.3 304.1 %all-to-all-start.1 = ((bf16[32,2,128,1024]{3,2,1,0:T(8,128)(2,1)}), bf16[32,2,128,1024]{3,2,1,0:T(8,128)(2,1)}, u32[]{:S(2)}, u32[]{:S(2)}) async-start(bf16[32,2,128,1024]{3,2,1,0:T(8,128)(2,1)} %bitcast.130), calls=%async_computation.1 | async-start | bytes 33554432 | tf_op jit(solution)/shard_map/all_to_all | solution.py:138
  652.3 21.0 %copy-start.1 = (bf16[8,384,128]{2,1,0:T(8,128)(2,1)S(1)}, bf16[8,384,128]{2,1,0:T(8,128)(2,1)}, u32[]{:S(2)}) copy-start(bf16[8,384,128]{2,1,0:T(8,128)(2,1)} %param.12) | copy-start | bytes 2359300
where the time goes:
time: 684 us; the launch traced here: 674 us
  waiting for transfers between devices  340 us (50%)
  local copies, waits for them, and re-layouts  244 us (36%)
  matrix products  65.2 us (10%)
  starting transfers between devices  12.6 us (2%)
  other arithmetic  10.5 us (2%)
    all_to_all x1, waiting for transfers between devices, on_device(): lax.all_to_all(outgoing, 'ping', split_axis=0, concat_axis=0, tiled=True)  296 us
    unnamed x21, local copies, waits for them, and re-layouts  82.5 us
    all_to_all x1, local copies, waits for them, and re-layouts, on_device(): lax.all_to_all(compressed, 'band', split_axis=3, concat_axis=0, tiled=True)  76.8 us
    convert_element_type x1, local copies, waits for them, and re-layouts, compress(): return total.reshape(pings, chans, 2, bins).astype(jnp.bfloat16)  48.6 us
    all_to_all x1, waiting for transfers between devices, on_device(): lax.all_to_all(compressed, 'band', split_axis=3, concat_axis=0, tiled=True)  44.8 us
    dot_general x1, matrix products, on_device(): jnp.dot(combiner, arrived.reshape(arrived.shape[0], -1), preferred_elemen...  16.6 us
  transfers between devices with their start and end apart: 2, of which 2 were waited for; matrix products, arithmetic and copies ran while one was open for 1% of the time, Pallas kernels for 0%

commit v1 on v0

--- a/solution.py
+++ b/solution.py
@@ -1,9 +1,25 @@
+import functools
 import jax
 import jax.numpy as jnp
 from jax import lax
 from jax.sharding import PartitionSpec as P
 
 SUB_PINGS = 8
+
+
+def rest_view_now(inner_x, which_axis):
+    return jnp.concatenate(
+        lax.all_to_all(
+            jnp.stack(jnp.split(inner_x, lax.axis_size(which_axis), axis=3), axis=0),
+            which_axis,
+            0,
+            0,
+        ),
+        axis=0,
+    )
+
+
+resolve_inputs_in = functools.partial(rest_view_now, which_axis="band")
 
 
 def toeplitz_blocks(replica):
@@ -106,7 +122,7 @@
     ping_index = lax.axis_index("ping")
     toeplitz = toeplitz_blocks(replica)
     compressed = compress(echoes, toeplitz)
-    band_tile = lax.all_to_all(compressed, "band", split_axis=3, concat_axis=0, tiled=True)
+    band_tile = resolve_inputs_in(compressed)
     beam_image = beamform(band_tile, steering, SUB_PINGS)
     blocks_here = beam_image.shape[0]
     capacity = max(2, (blocks_here + ping_count - 1) // ping_count)

time: 684 us -> 522 us (0.76)
  local copies, waits for them, and re-layouts: 244 us -> 85.9 us
    all_to_all x1, local copies, waits for them, and re-layouts: 76.8 us -> 8.57 us  [rest_view_now(): lax.all_to_all(jnp.stack(jnp.split(inner_x, lax.axis_size(which_axis), ax...]
    unnamed x21 -> x26, local copies, waits for them, and re-layouts: 82.5 us -> 32.1 us
    convert_element_type x1, local copies, waits for them, and re-layouts: 48.6 us -> 7.31 us  [compress(): return total.reshape(pings, chans, 2, bins).astype(jnp.bfloat16)]
    another operation x0 -> x2, local copies, waits for them, and re-layouts: none -> 9.1 us  [the longest x1 7.22 us: beamform(): grouped = tile.reshape(blocks, sub_pings * chans * parts, bins)]
    reshape x1 -> x0, local copies, waits for them, and re-layouts: 7.22 us -> none  [beamform(): grouped = tile.reshape(blocks, sub_pings * chans * parts, bins)]
where the time goes in v1:
time: 522 us; the launch traced here: 516 us
  waiting for transfers between devices  341 us (65%)
  local copies, waits for them, and re-layouts  85.9 us (16%)
  matrix products  65.4 us (13%)
  starting transfers between devices  12.8 us (2%)
  other arithmetic  10.5 us (2%)
    all_to_all x1, waiting for transfers between devices, on_device(): lax.all_to_all(outgoing, 'ping', split_axis=0, concat_axis=0, tiled=True)  296 us
    all_to_all x1, waiting for transfers between devices, rest_view_now(): lax.all_to_all(jnp.stack(jnp.split(inner_x, lax.axis_size(which_axis), ax...  44.8 us
    unnamed x26, local copies, waits for them, and re-layouts  32.1 us
    dot_general x1, matrix products, on_device(): jnp.dot(combiner, arrived.reshape(arrived.shape[0], -1), preferred_elemen...  16.6 us
    dot_general x1, matrix products, pack_rows(): jnp.dot(packer, source.reshape(source.shape[0], -1), preferred_element_ty...  13.6 us
    dot_general x1, matrix products, range_interp(): product = jnp.dot(flat, dense, preferred_element_type=jnp.float32)  12.6 us
  transfers between devices with their start and end apart: 2, of which 2 were waited for; matrix products, arithmetic and copies ran while one was open for 1% of the time, Pallas kernels for 0%

profile of v1, /device:TPU:68, one launch (start us, length us, event | category | flops | bytes accessed | tf_op | source)
XLA Modules:
  0.0 516.0 jit_solution(7477339273675361191)
XLA Ops:
  6.3 9.8 %maximum_maximum_fusion = bf16[8,512,256]{2,0,1:T(8,128)(2,1)S(1)} fusion(bf16[8,128,128]{2,0,1:T(8,128)(2,1)S(1)} %fusion.27, bf16[8,128,128]{2,0,1:T(8,128)(2,1)S(1)} %get-tuple-element.21, bf16[8,128,128]{2,0,1:T(8,128)(2,1)S(1)} %get-tuple-element.22, bf16[8,128,128]{2,0,1:T(8,128)(2,1)S(1)} %fusion.28, bf16[8,128,128]{2,0,1:T(8,128)(2,1)S(1)} %get-tuple-element.10, ...), kind=kLoop, calls=%fused_computation.26 | loop fusion | flops 16777216 | bytes 3670016 | tf_op jit(solution)/shard_map/concatenate | solution.py:47
  16.5 7.8 %reshape.184 = bf16[16,8,2,64,128]{4,3,2,1,0:T(8,128)(2,1)} reshape(bf16[16,8,2,8192]{3,2,1,0:T(2,128)(2,1)} %param.8) | data formatting | bytes 8388608 | tf_op jit(solution)/shard_map/reshape | solution.py:54
  24.3 6.7 %fusion.15 = f32[16,8,2,64,128]{4,3,0,2,1:T(8,128)} fusion(bf16[8,1,2,128,2,128]{5,0,4,3,2,1:T(8,128)(2,1)S(1)} %get-tuple-element.8, bf16[16,8,2,64,128]{4,3,2,1,0:T(8,128)(2,1)} %reshape.184), kind=kOutput, calls=%fused_computation.21 | convolution fusion | flops 1073741824 | bytes 13631488 | tf_op jit(solution)/shard_map/pcqbk,cqkon->pcobn/dot_general | solution.py:59
  31.0 4.7 slice.38
  35.6 2.9 fusion.2
  38.6 7.3 %convert_element_type.87 = bf16[16,8,2,8192]{3,0,2,1:T(8,128)(2,1)} reshape(bf16[16,8,2,64,128]{4,3,0,2,1:T(8,128)(2,1)} %fusion.2) | data formatting | bytes 8388608 | tf_op jit(solution)/shard_map/convert_element_type | solution.py:64
  45.9 1.9 fusion.37
  47.8 1.9 fusion.36
  49.6 1.9 fusion.35
  60.9 4.9 all-to-all-start
  68.0 2.7 copy.32
  70.7 44.8 %all-to-all-done = bf16[8,16,8,2,1024]{4,1,3,2,0:T(8,128)(2,1)} async-done(((bf16[8,16,8,2,1024]{4,1,3,2,0:T(8,128)(2,1)}), bf16[8,16,8,2,1024]{4,1,3,2,0:T(8,128)(2,1)}, u32[]{:S(2)}, u32[]{:S(2)}) %all-to-all-start) | async-done | bytes 4194336 | tf_op jit(solution)/shard_map/all_to_all | solution.py:12
  115.5 8.6 %copy.26 = bf16[8,16,8,2,1024]{4,3,2,1,0:T(2,128)(2,1)} copy(bf16[8,16,8,2,1024]{4,1,3,2,0:T(8,128)(2,1)} %all-to-all-done) | data formatting | bytes 8388608 | tf_op jit(solution)/shard_map/all_to_all | solution.py:12
  124.0 7.2 %reshape_reshape.6 = bf16[16,128,1024]{2,1,0:T(8,128)(2,1)} reshape(bf16[8,16,8,2,1024]{4,3,2,1,0:T(2,128)(2,1)} %copy.26) | data formatting | bytes 8388608 | tf_op jit(solution)/shard_map/reshape;reshape | solution.py:70
  131.3 3.7 convolution_convert_fusion.3
  135.0 2.4 convolution_convert_fusion.2
  137.4 12.6 %convolution_convert_fusion.1 = bf16[4096,1024]{1,0:T(8,128)(2,1)} fusion(bf16[4096,1024]{1,0:T(8,128)(2,1)S(1)} %bitcast.162, bf16[128,8,8,128]{3,2,1,0:T(8,128)(2,1)} %bitcast.164), kind=kOutput, calls=%fused_computation.11 | convolution fusion | flops 8594128896 | bytes 18874368 | tf_op jit(solution)/shard_map/dot_general | solution.py:109
  150.1 8.0 %reshape_reshape.7 = bf16[16,262144]{1,0:T(8,128)(2,1)} reshape(bf16[4096,1024]{1,0:T(8,128)(2,1)} %convolution_convert_fusion.1) | data formatting | bytes 16777216 | tf_op jit(solution)/shard_map/reshape;reshape | solution.py:114
  158.0 13.6 %convolution_convert_fusion = bf16[32,262144]{1,0:T(8,128)(2,1)} fusion(pred[32,16]{1,0:T(32,128)(4,1)S(1)} %and.49, bf16[16,262144]{1,0:T(8,128)(2,1)} %reshape_reshape.7), kind=kOutput, calls=%fused_computation | convolution fusion | flops 276824064 | bytes 25166336 | tf_op jit(solution)/shard_map/dot_general | solution.py:114
  171.6 18.7 %copy.59 = bf16[4,8,256,1024]{3,2,1,0:T(8,128)(2,1)} copy(bf16[4,8,256,1024]{3,1,2,0:T(8,128)(2,1)} %bitcast.160) | data formatting | bytes 33554432
  190.3 7.9 %all-to-all-start.1 = ((bf16[32,2,128,1024]{3,2,1,0:T(8,128)(2,1)}), bf16[32,2,128,1024]{3,2,1,0:T(8,128)(2,1)}, u32[]{:S(2)}, u32[]{:S(2)}) async-start(bf16[32,2,128,1024]{3,2,1,0:T(8,128)(2,1)} %bitcast.159), calls=%async_computation.1 | async-start | bytes 33554432 | tf_op jit(solution)/shard_map/all_to_all | solution.py:154
  198.7 295.9 %all-to-all-done.1 = bf16[32,2,128,1024]{3,2,1,0:T(8,128)(2,1)} async-done(((bf16[32,2,128,1024]{3,2,1,0:T(8,128)(2,1)}), bf16[32,2,128,1024]{3,2,1,0:T(8,128)(2,1)}, u32[]{:S(2)}, u32[]{:S(2)}) %all-to-all-start.1) | async-done | bytes 16777248 | tf_op jit(solution)/shard_map/all_to_all | solution.py:154
  494.6 16.6 %fusion.20 = bf16[8,2,128,1024]{3,0,2,1:T(8,128)(2,1)S(1)} fusion(bf16[8,32,1,1]{0,1,3,2:T(8,128)(2,1)S(1)} %bitcast.169, bf16[2,128,1024,32]{2,1,0,3:T(8,128)(2,1)} %bitcast.83), kind=kOutput, calls=%fused_computation.22 | convolution fusion | flops 136314880 | bytes 20972032 | tf_op jit(solution)/shard_map/dot_general | solution.py:155
  511.2 4.4 copy.35
  (54 shorter events, 18.5 us)
Async XLA Ops:
  0.0 66.7 %copy-start = (bf16[8,384,128]{2,1,0:T(8,128)(2,1)S(1)}, bf16[8,384,128]{2,1,0:T(8,128)(2,1)}, u32[]{:S(2)}) copy-start(bf16[8,384,128]{2,1,0:T(8,128)(2,1)} %param.12) | copy-start | bytes 2359300
  31.0 4.7 copy-start.2
  60.9 4.9 copy-start.5
  60.9 5.3 %copy-start.3 = (bf16[2,64,64]{2,1,0:T(8,128)(2,1)S(1)}, bf16[2,64,64]{2,1,0:T(8,128)(2,1)}, u32[]{:S(2)}) copy-start(bf16[2,64,64]{2,1,0:T(8,128)(2,1)} %param.10) | copy-start | bytes 49156
  60.9 5.7 %copy-start.7 = (s32[8]{0:T(128)S(1)}, s32[8]{0:T(128)}, u32[]{:S(2)}) copy-start(s32[8]{0:T(128)} %param.13) | copy-start | bytes 100
  60.9 54.5 %all-to-all-start = ((bf16[8,16,8,2,1024]{4,1,3,2,0:T(8,128)(2,1)}), bf16[8,16,8,2,1024]{4,1,3,2,0:T(8,128)(2,1)}, u32[]{:S(2)}, u32[]{:S(2)}) async-start(bf16[8,16,8,2,1024]{4,1,3,2,0:T(8,128)(2,1)} %fusion.30), calls=%async_computation | async-start | bytes 8388608 | tf_op jit(solution)/shard_map/all_to_all | solution.py:12
  65.8 4.9 copy-start.4
  190.3 8.1 %copy-start.6 = (s32[256]{0:T(256)S(1)}, s32[256]{0:T(256)}, u32[]{:S(2)}) copy-start(s32[256]{0:T(256)} %param.15) | copy-start | bytes 3076
  190.3 304.2 %all-to-all-start.1 = ((bf16[32,2,128,1024]{3,2,1,0:T(8,128)(2,1)}), bf16[32,2,128,1024]{3,2,1,0:T(8,128)(2,1)}, u32[]{:S(2)}, u32[]{:S(2)}) async-start(bf16[32,2,128,1024]{3,2,1,0:T(8,128)(2,1)} %bitcast.159), calls=%async_computation.1 | async-start | bytes 33554432 | tf_op jit(solution)/shard_map/all_to_all | solution.py:154
  494.6 21.0 %copy-start.1 = (bf16[8,384,128]{2,1,0:T(8,128)(2,1)S(1)}, bf16[8,384,128]{2,1,0:T(8,128)(2,1)}, u32[]{:S(2)}) copy-start(bf16[8,384,128]{2,1,0:T(8,128)(2,1)} %param.12) | copy-start | bytes 2359300
